TPU v7x, 32 devices: a whole 2x2x4 slice. The times are simulated.
32 devices in a mesh: genome: 4 (over z), trow: 2 (over core), tcol: 4 (over y, x).
Axes of the slice: x: 2, y: 2, z: 4, core: 2. Of those that a mesh axis runs over, the one named last changes fastest.
Arguments:
- ldscore: float32 [4096], P('genome'), may hold values from 1 to 100
- zscores: bfloat16 [4096, 4096], P('genome', ('trow', 'tcol')), may hold values from -30 to 30
Outputs:
- rg: float32 [2, 2048, 2, 2048], P('trow', 'genome', None, 'tcol')
- rg_se: float32 [2, 2048, 2, 2048], P('trow', 'genome', None, 'tcol')
All inputs are finite; a program needn't handle non-finite values.
Results may differ from a plain program's by a relative error of at most 0.038.
Values may be sent and summed in bfloat16 or wider, within the bound.
No kernel may reach another device: no remote copies, remote signals or barrier semaphores. Data moves between devices by JAX's collectives and lax.ppermute only.
A program may use at most 192 MiB of HBM per device.

v0:
```python
import jax
import jax.numpy as jnp
from jax import lax
from jax.sharding import PartitionSpec as P

floor_value = 0.002


def contract(left, right):
    return lax.dot_general(
        left, right, (((0,), (0,)), ((), ())), preferred_element_type=jnp.float32
    )


def slope_fit(inv_sum, ld_sum, y_sum, l_sum, count):
    return (inv_sum * l_sum - count * y_sum) / (inv_sum * ld_sum - count * count)


def weights_for(herit_pos, ld_column):
    return (1.0 / (1.0 + herit_pos[None, :] * ld_column[:, None])).astype(jnp.bfloat16)


def coupling(tiles):
    return (tiles[2] * tiles[1] - tiles[3] * tiles[0]) / (tiles[2] * tiles[4] - tiles[3] * tiles[3])


def per_device(ldscore, zscores):
    blocks = lax.axis_size("genome")
    grid_rows = lax.axis_size("trow")
    grid_cols = lax.axis_size("tcol")
    snp_count = zscores.shape[0]
    shard_width = zscores.shape[1]
    traits = shard_width * grid_rows * grid_cols
    row_width = traits // grid_rows
    row_share = row_width // blocks
    row_index = lax.axis_index("trow")
    col_index = lax.axis_index("tcol")
    genome_index = lax.axis_index("genome")
    ld_weight = 1.0 / ldscore
    z_float = zscores.astype(jnp.float32)
    z_square = z_float * z_float
    own_stats = jnp.stack(
        [jnp.sum(z_square * ld_weight[:, None], axis=0), jnp.sum(z_square, axis=0)]
    )
    own_scalars = jnp.stack([jnp.sum(ld_weight), jnp.sum(ldscore)])
    all_stats, all_scalars = (
        lax.all_gather(own_stats[None], ("genome", "trow", "tcol"), axis=0, tiled=True),
        lax.all_gather(own_scalars[None], ("genome", "trow", "tcol"), axis=0, tiled=True),
    )
    all_stats = all_stats.reshape(blocks, grid_rows * grid_cols, 2, shard_width)
    all_stats = all_stats.transpose(0, 2, 1, 3).reshape(blocks, 2, traits)
    all_scalars = all_scalars.reshape(blocks, grid_rows * grid_cols, 2)[:, 0, :]
    total_stats = jnp.sum(all_stats, axis=0)
    total_scalars = jnp.sum(all_scalars, axis=0)
    herit_full = slope_fit(
        total_scalars[0],
        total_scalars[1],
        total_stats[0],
        total_stats[1],
        float(snp_count * blocks),
    )
    rest_stats = total_stats[None] - all_stats
    rest_scalars = total_scalars[None] - all_scalars
    herit_del = slope_fit(
        rest_scalars[:, 0:1],
        rest_scalars[:, 1:2],
        rest_stats[:, 0],
        rest_stats[:, 1],
        float(snp_count * (blocks - 1)),
    )
    herit_pos = jnp.maximum(herit_full, 0.0)
    col_z = lax.all_gather(zscores, "trow", axis=1, tiled=True)
    col_herit = lax.dynamic_index_in_dim(
        herit_pos.reshape(grid_rows, grid_cols, shard_width), col_index, 1, keepdims=False
    ).reshape(-1)
    col_u = weights_for(col_herit, ldscore)
    col_zu = (col_z.astype(jnp.float32) * col_u.astype(jnp.float32)).astype(jnp.bfloat16)
    piece = lax.all_gather(zscores, "tcol", axis=1, tiled=True)
    herit_rows = lax.dynamic_slice_in_dim(herit_pos, row_index * row_width, piece.shape[1])
    row_u = weights_for(herit_rows, ldscore)
    u_float = row_u.astype(jnp.float32)
    scaled = piece.astype(jnp.float32) * u_float
    row_zu = scaled.astype(jnp.bfloat16)
    row_scaled = (scaled * ld_weight[:, None]).astype(jnp.bfloat16)
    products = [contract(row_scaled, col_zu), contract(row_zu, col_zu)]
    row_inv = (u_float * ld_weight[:, None]).astype(jnp.bfloat16)
    row_ld = (u_float * ldscore[:, None]).astype(jnp.bfloat16)
    products = products + [
        contract(row_inv, col_u),
        contract(row_u, col_u),
        contract(row_ld, col_u),
    ]
    sums = jnp.stack(products)
    sums = sums.astype(jnp.bfloat16)[:, None]
    row_start = row_index * row_width + genome_index * row_share
    tiles = lax.all_to_all(sums, "genome", split_axis=2, concat_axis=1, tiled=True)
    tile_values = tiles.astype(jnp.float32)
    totals = jnp.sum(tile_values, axis=1)
    deleted = totals[:, None] - tile_values
    full_g = coupling(totals)
    del_g = coupling(deleted)
    herit_floor = jnp.maximum(herit_full, floor_value)
    del_floor = jnp.maximum(herit_del, floor_value)
    rows_full = lax.dynamic_slice_in_dim(herit_floor, row_start, row_share)
    cols_full = lax.dynamic_index_in_dim(
        herit_floor.reshape(grid_rows, grid_cols, shard_width), col_index, 1, keepdims=False
    ).reshape(-1)
    rows_del = lax.dynamic_slice_in_dim(del_floor, row_start, row_share, axis=1)
    cols_del = lax.dynamic_index_in_dim(
        del_floor.reshape(blocks, grid_rows, grid_cols, shard_width), col_index, 2, keepdims=False
    ).reshape(blocks, -1)
    rg_tile = full_g / jnp.sqrt(rows_full[:, None] * cols_full[None, :])
    rg_del = del_g / jnp.sqrt(rows_del[:, :, None] * cols_del[:, None, :])
    mean_del = jnp.mean(rg_del, axis=0)
    differ = rg_del - mean_del[None]
    spread = jnp.sum(differ * differ, axis=0)
    se_tile = jnp.sqrt((blocks - 1) / blocks * spread)
    out_shape = (1, row_share, grid_rows, shard_width)
    return (rg_tile.reshape(out_shape), se_tile.reshape(out_shape))


def solution(mesh):
    return jax.shard_map(
        per_device,
        mesh=mesh,
        in_specs=(P("genome"), P("genome", ("trow", "tcol"))),
        out_specs=(P("trow", "genome", None, "tcol"), P("trow", "genome", None, "tcol")),
        check_vma=False,
    )
```

profile of v0, /device:TPU:0, one launch (start us, length us, event | category | flops | bytes accessed | tf_op | source)
XLA Modules:
  0.0 1032.2 jit_solution(11515729871586139848)
XLA Ops:
  7.2 0.0 all-gather.8.cloned.1.call-start
  7.2 0.7 all-gather.8.cloned.1.call-update
  7.9 0.0 all-gather.6.cloned.1.call-start
  7.9 0.7 all-gather.6.cloned.1.call-update
  8.7 1.3 fusion.41
  10.0 1.5 maximum_dynamic-update-slice_fusion
  11.4 42.1 %all-reduce = f32[64]{0:T(128)S(1)} all-reduce(f32[64]{0:T(128)S(1)} %maximum_dynamic-update-slice_fusion), channel_id=2, replica_groups=mesh['genome'=4,'trow'=2,'tcol'=4] {'genome','trow','tcol'}, use_global_device_ids=true, to_apply=%add | all-reduce | flops 64 | bytes 512
  53.5 0.1 reshape.288
  53.6 0.6 fusion.49
  55.5 1.6 multiply_reduce_fusion.1
  57.2 67.2 %all-gather.2 = f32[32,2,512]{2,1,0:T(2,128)S(1)} all-gather(f32[1,2,512]{2,1,0:T(2,128)S(1)} %maximum_bitcast_fusion), channel_id=3, replica_groups=mesh['genome'=4,'trow'=2,'tcol'=4] {'genome','trow','tcol'}, dimensions={0}, use_global_device_ids=true | all-gather | bytes 135168 | tf_op jit(solution)/shard_map/all_gather | solution.py:47
  124.4 0.7 fusion.40
  125.2 0.0 all-gather.8.cloned.1.call-done
  125.2 0.0 all-gather.6.cloned.1.call-done
  125.2 0.0 copy-start.1
  125.2 0.0 copy-start.2
  125.3 0.0 copy-start.3
  125.3 10.8 %bitcast_dynamic-update-slice_fusion.4 = bf16[5,1,2048,1024]{3,2,1,0:T(8,128)(2,1)} fusion(bf16[1024,2048]{1,0:T(8,128)(2,1)} %all-gather.6.cloned.1.call-done, f32[1024]{0:T(1024)S(1)} %get-tuple-element.21, f32[1024]{0:T(1024)} %param.2, f32[2048]{0:T(1024)S(1)} %dynamic_slice.20, bf16[1024,1024]{1,0:T(8,128)(2,1)} %all-gather.8.cloned.1.call-done, ...), kind=kOutput, calls=%fused_computation.27 | convolution fusion | flops 4324327424 | bytes 10510336 | tf_op jit(solution)/shard_map/dot_general | solution.py:10
  136.1 0.0 copy-done.2
  136.1 7.8 bitcast_dynamic-update-slice_fusion.3
  143.9 7.7 bitcast_dynamic-update-slice_fusion.2
  151.6 6.9 bitcast_dynamic-update-slice_fusion.1
  158.5 6.8 bitcast_dynamic-update-slice_fusion
  165.3 23.9 %copy.21 = bf16[5,1,2048,1024]{3,0,1,2:T(8,128)(2,1)} copy(bf16[5,1,2048,1024]{3,2,1,0:T(8,128)(2,1)} %bitcast_dynamic-update-slice_fusion) | data formatting | bytes 41943040 | tf_op jit(solution)/shard_map/stack | solution.py:93
  189.2 9.9 all-to-all-start
  199.2 0.1 reshape.290
  199.3 0.1 copy.23
  199.5 0.5 broadcast.132
  200.0 1.1 slice_multiply_fusion.6
  201.1 0.1 mul.285
  201.1 0.1 squeeze.18
  201.2 0.1 bitcast_subtract_fusion
  201.3 0.1 maximum_reduce_fusion
  201.5 0.1 dynamic_slice.22
  201.6 0.1 copy_bitcast_fusion.1
  201.7 0.1 fusion.33
  201.8 715.7 %all-to-all-done = bf16[5,1,2048,1024]{3,0,1,2:T(8,128)(2,1)} async-done(((bf16[5,1,2048,1024]{3,0,1,2:T(8,128)(2,1)}), bf16[5,1,2048,1024]{3,0,1,2:T(8,128)(2,1)}, u32[]{:S(2)}, u32[]{:S(2)}) %all-to-all-start) | async-done | bytes 20971552 | tf_op jit(solution)/shard_map/all_to_all | solution.py:96
  917.5 26.6 %copy.22 = bf16[5,1,2048,1024]{3,2,0,1:T(8,128)(2,1)} copy(bf16[5,1,2048,1024]{3,0,1,2:T(8,128)(2,1)} %all-to-all-done) | data formatting | bytes 41943040 | tf_op jit(solution)/shard_map/all_to_all | solution.py:96
  944.1 16.0 %convert_reduce_fusion = f32[5,512,1024]{2,1,0:T(8,128)} fusion(bf16[5,4,512,1024]{3,2,1,0:T(8,128)(2,1)} %bitcast.61), kind=kLoop, calls=%fused_computation.1 | loop fusion | flops 18350080 | bytes 31457280 | tf_op jit(solution)/shard_map/reduce_sum | solution.py:98
  960.1 28.2 %convert_subtract_fusion = f32[5,4,512,1024]{3,2,1,0:T(8,128)} fusion(bf16[5,4,512,1024]{3,2,1,0:T(8,128)(2,1)} %bitcast.62, f32[5,512,1024]{2,1,0:T(8,128)} %convert_reduce_fusion), kind=kLoop, calls=%fused_computation | loop fusion | flops 20971520 | bytes 73400320 | tf_op jit(solution)/shard_map/sub | solution.py:99
  988.3 2.6 fusion.26
  990.8 20.1 %fusion.44 = (f32[512,1024]{1,0:T(8,128)S(1)}, f32[4,512,1024]{2,1,0:T(8,128)}) fusion(f32[4,1024]{1,0:T(4,128)S(1)} %bitcast.71, f32[4,512]{1,0:T(4,128)S(1)} %fusion.33, f32[5,4,512,1024]{3,2,1,0:T(8,128)} %convert_subtract_fusion), kind=kLoop, calls=%fused_computation.85 | loop fusion | flops 20447232 | bytes 52453376 | tf_op jit(solution)/shard_map/reduce_sum | solution.py:114
  1011.0 0.2 broadcast_multiply_fusion
  1011.1 5.1 multiply_reduce_fusion
  1016.2 0.5 multiply_sqrt_fusion
  1016.7 2.8 sqrt.22
  1019.5 3.0 div.75
  1022.6 2.6 rsqrt_multiply_fusion
  (23 shorter events, 0.3 us)
Async XLA Ops:
  7.2 118.0 %all-gather.8.cloned.1.call-start = ((), (), s32[]{:S(2)}) async-start(), calls=%async_computation.2 | async-start | bytes 3145728 | tf_op jit(solution)/shard_map/all_gather | solution.py:72
  7.9 117.3 %all-gather.6.cloned.1.call-start = ((), (), s32[]{:S(2)}) async-start(), calls=%async_computation.1 | async-start | bytes 5242880 | tf_op jit(solution)/shard_map/all_gather | solution.py:78
  125.2 10.9 %copy-start.1 = (f32[1024]{0:T(1024)S(1)}, f32[1024]{0:T(1024)}, u32[]{:S(2)}) copy-start(f32[1024]{0:T(1024)} %param.2) | copy-start | bytes 12292
  125.2 10.9 %copy-start.2 = (bf16[1024,2048]{1,0:T(8,128)(2,1)S(1)}, bf16[1024,2048]{1,0:T(8,128)(2,1)}, u32[]{:S(2)}) copy-start(bf16[1024,2048]{1,0:T(8,128)(2,1)} %all-gather.6.cloned.1.call-done) | copy-start | bytes 12582916
  125.3 10.9 %copy-start.3 = (bf16[1024,1024]{1,0:T(8,128)(2,1)S(1)}, bf16[1024,1024]{1,0:T(8,128)(2,1)}, u32[]{:S(2)}) copy-start(bf16[1024,1024]{1,0:T(8,128)(2,1)} %all-gather.8.cloned.1.call-done) | copy-start | bytes 6291460
  189.2 728.2 %all-to-all-start = ((bf16[5,1,2048,1024]{3,0,1,2:T(8,128)(2,1)}), bf16[5,1,2048,1024]{3,0,1,2:T(8,128)(2,1)}, u32[]{:S(2)}, u32[]{:S(2)}) async-start(bf16[5,1,2048,1024]{3,0,1,2:T(8,128)(2,1)} %copy.21), calls=%async_computation | async-start | bytes 67108864 | tf_op jit(solution)/shard_map/all_to_all | solution.py:96
  960.1 28.2 %copy-start = (f32[5,512,1024]{2,1,0:T(8,128)S(1)}, f32[5,512,1024]{2,1,0:T(8,128)}, u32[]{:S(2)}) copy-start(f32[5,512,1024]{2,1,0:T(8,128)} %convert_reduce_fusion) | copy-start | bytes 31457284
Sparse Core Ops, SparseCore 0:
  9.5 13.2 all-gather.7
  24.7 54.7 all-gather.5
where the time goes:
time: 1040 us; the launch traced here: 1030 us
  waiting for transfers between devices  717 us (69%)
  blocking collectives  109 us (10%)
  other arithmetic  81.7 us (8%)
  local copies, waits for them, and re-layouts  58.2 us (6%)
  matrix products  40 us (4%)
  between operations  15.8 us (2%)
    all_to_all x1, waiting for transfers between devices, per_device(): lax.all_to_all(sums, 'genome', split_axis=2, concat_axis=1, tiled=True)  716 us
    all_gather x1, blocking collectives, per_device(): lax.all_gather(own_stats[None], ('genome', 'trow', 'tcol'), axis=0, tiled...  67.2 us
    unnamed x1, blocking collectives  42.1 us
    dot_general x5, matrix products, contract(): lax.dot_general(left, right, (((0,), (0,)), ((), ())), preferred_element_...  40 us
    sub x1, other arithmetic, per_device(): deleted = totals[:, None] - tile_values  28.2 us
    all_to_all x1, local copies, waits for them, and re-layouts, per_device(): lax.all_to_all(sums, 'genome', split_axis=2, concat_axis=1, tiled=True)  26.6 us
    another operation x1, local copies, waits for them, and re-layouts, per_device(): sums = jnp.stack(products)  23.9 us
  transfers between devices with their start and end apart: 3, of which 1 were waited for; matrix products, arithmetic and copies ran while one was open for 1% of the time, Pallas kernels for 0%

commit v1 on v0

--- a/solution.py
+++ b/solution.py
@@ -93,7 +93,15 @@
     sums = jnp.stack(products)
     sums = sums.astype(jnp.bfloat16)[:, None]
     row_start = row_index * row_width + genome_index * row_share
-    tiles = lax.all_to_all(sums, "genome", split_axis=2, concat_axis=1, tiled=True)
+    tiles = jnp.concatenate(
+        lax.all_to_all(
+            jnp.stack(jnp.split(sums, lax.axis_size("genome"), 2), axis=0),
+            axis_name="genome",
+            split_axis=0,
+            concat_axis=0,
+        ),
+        1,
+    )
     tile_values = tiles.astype(jnp.float32)
     totals = jnp.sum(tile_values, axis=1)
     deleted = totals[:, None] - tile_values

time: 1040 us -> 739 us (0.71)
  waiting for transfers between devices: 717 us -> 448 us
  local copies, waits for them, and re-layouts: 58.2 us -> 18.7 us
    all_to_all x1, waiting for transfers between devices: 716 us -> 446 us  [per_device(): lax.all_to_all(jnp.stack(jnp.split(sums, lax.axis_size('genome'), 2), axi...]
    all_to_all x1 -> x0, local copies, waits for them, and re-layouts: 26.6 us -> none  [per_device(): lax.all_to_all(sums, 'genome', split_axis=2, concat_axis=1, tiled=True)]
    another operation x1 -> x2, local copies, waits for them, and re-layouts: 23.9 us -> 10.3 us  [per_device(): jnp.stack(jnp.split(sums, lax.axis_size('genome'), 2), axis=0)]
where the time goes in v1:
time: 739 us; the launch traced here: 729 us
  waiting for transfers between devices  448 us (61%)
  blocking collectives  109 us (15%)
  other arithmetic  90 us (12%)
  matrix products  39.7 us (5%)
  local copies, waits for them, and re-layouts  18.7 us (3%)
  between operations  16 us (2%)
  starting transfers between devices  8.04 us (1%)
    all_to_all x1, waiting for transfers between devices, per_device(): lax.all_to_all(jnp.stack(jnp.split(sums, lax.axis_size('genome'), 2), axi...  446 us
    all_gather x1, blocking collectives, per_device(): lax.all_gather(own_stats[None], ('genome', 'trow', 'tcol'), axis=0, tiled...  67.3 us
    unnamed x1, blocking collectives  42.1 us
    dot_general x5, matrix products, contract(): lax.dot_general(left, right, (((0,), (0,)), ((), ())), preferred_element_...  39.7 us
    sub x1, other arithmetic, per_device(): deleted = totals[:, None] - tile_values  23.2 us
    reduce_sum x1, other arithmetic, per_device(): mean_del = jnp.mean(rg_del, axis=0)  19.9 us
    reduce_sum x1, other arithmetic, per_device(): totals = jnp.sum(tile_values, axis=1)  16 us
  transfers between devices with their start and end apart: 3, of which 1 were waited for; matrix products, arithmetic and copies ran while one was open for 1% of the time, Pallas kernels for 0%

profile of v1, /device:TPU:0, one launch (start us, length us, event | category | flops | bytes accessed | tf_op | source)
XLA Modules:
  0.0 729.3 jit_solution(6737334093491915948)
XLA Ops:
  7.2 0.0 all-gather.8.cloned.1.call-start
  7.2 0.7 all-gather.8.cloned.1.call-update
  7.9 0.0 all-gather.6.cloned.1.call-start
  7.9 0.7 all-gather.6.cloned.1.call-update
  8.7 1.3 fusion.41
  10.0 1.5 maximum_dynamic-update-slice_fusion
  11.4 42.1 %all-reduce = f32[64]{0:T(128)S(1)} all-reduce(f32[64]{0:T(128)S(1)} %maximum_dynamic-update-slice_fusion), channel_id=2, replica_groups=mesh['genome'=4,'trow'=2,'tcol'=4] {'genome','trow','tcol'}, use_global_device_ids=true, to_apply=%add | all-reduce | flops 64 | bytes 512
  53.5 0.1 reshape.286
  53.6 1.6 multiply_reduce_fusion.1
  55.3 67.3 %all-gather.2 = f32[32,2,512]{2,1,0:T(2,128)S(1)} all-gather(f32[1,2,512]{2,1,0:T(2,128)S(1)} %maximum_bitcast_fusion), channel_id=3, replica_groups=mesh['genome'=4,'trow'=2,'tcol'=4] {'genome','trow','tcol'}, dimensions={0}, use_global_device_ids=true | all-gather | bytes 135168 | tf_op jit(solution)/shard_map/all_gather | solution.py:47
  122.6 0.6 fusion.51
  124.5 0.7 broadcast_maximum_fusion
  125.2 0.1 fusion.43
  125.4 0.0 all-gather.8.cloned.1.call-done
  125.4 0.0 all-gather.6.cloned.1.call-done
  125.4 0.0 copy-start.1
  125.4 10.8 %bitcast_dynamic-update-slice_fusion.4 = bf16[5,1,2048,1024]{3,2,1,0:T(8,128)(2,1)} fusion(bf16[1024,2048]{1,0:T(8,128)(2,1)} %all-gather.6.cloned.1.call-done, f32[1024]{0:T(1024)S(1)} %get-tuple-element.24, f32[1024]{0:T(1024)} %param.2, f32[2048]{0:T(1024)S(1)} %dynamic_slice.20, bf16[1024,1024]{1,0:T(8,128)(2,1)} %all-gather.8.cloned.1.call-done, ...), kind=kOutput, calls=%fused_computation.34 | convolution fusion | flops 4324327424 | bytes 10510336 | tf_op jit(solution)/shard_map/dot_general | solution.py:10
  136.3 7.8 %bitcast_dynamic-update-slice_fusion.3 = bf16[5,1,2048,1024]{3,2,1,0:T(8,128)(2,1)} fusion(bf16[5,1,2048,1024]{3,2,1,0:T(8,128)(2,1)} %bitcast_dynamic-update-slice_fusion.4, bf16[1024,2048]{1,0:T(8,128)(2,1)S(1)} %copy-done.2, f32[1024]{0:T(1024)S(1)} %copy-done.1, f32[2048]{0:T(1024)S(1)} %dynamic_slice.20, bf16[1024,1024]{1,0:T(8,128)(2,1)S(1)} %copy-done.3, ...), kind=kOutput, calls=%fused_computation.33 | convolution fusion | flops 4322230272 | bytes 10506240 | tf_op jit(solution)/shard_map/dot_general | solution.py:10
  144.1 7.4 %bitcast_dynamic-update-slice_fusion.2 = bf16[5,1,2048,1024]{3,2,1,0:T(8,128)(2,1)} fusion(bf16[5,1,2048,1024]{3,2,1,0:T(8,128)(2,1)} %bitcast_dynamic-update-slice_fusion.3, f32[1024]{0:T(1024)S(1)} %get-tuple-element.24, f32[1024]{0:T(1024)S(1)} %copy-done.1, f32[2048]{0:T(1024)S(1)} %dynamic_slice.20, f32[1024]{0:T(1024)S(1)} %bitcast.90), kind=kOutput, calls=%fused_computation.32 | convolution fusion | flops 4315938816 | bytes 4218880 | tf_op jit(solution)/shard_map/dot_general | solution.py:10
  151.5 6.9 bitcast_dynamic-update-slice_fusion.1
  158.3 6.8 bitcast_dynamic-update-slice_fusion
  165.2 3.1 slice_bitcast_fusion
  168.2 7.2 slice_bitcast_fusion.3
  175.5 8.8 %pad_maximum_fusion = bf16[4,5,1,512,1024]{4,3,1,2,0:T(8,128)(2,1)} fusion(bf16[1,5,1,512,1024]{4,3,1,2,0:T(8,128)(2,1)S(1)} %slice_bitcast_fusion, bf16[1,5,1,512,1024]{4,3,1,2,0:T(8,128)(2,1)S(1)} %get-tuple-element.15, bf16[1,5,1,512,1024]{4,3,1,2,0:T(8,128)(2,1)S(1)} %get-tuple-element.16, bf16[1,5,1,512,1024]{4,3,1,2,0:T(8,128)(2,1)S(1)} %get-tuple-element.14), kind=kLoop, calls=%fused_computation.4 | loop fusion | flops 31457280 | bytes 41943040 | tf_op jit(solution)/shard_map/stack | solution.py:98
  184.3 8.0 %all-to-all-start = ((bf16[4,5,1,512,1024]{4,3,1,2,0:T(8,128)(2,1)}), bf16[4,5,1,512,1024]{4,3,1,2,0:T(8,128)(2,1)}, u32[]{:S(2)}, u32[]{:S(2)}) async-start(bf16[4,5,1,512,1024]{4,3,1,2,0:T(8,128)(2,1)} %pad_maximum_fusion), calls=%async_computation | async-start | bytes 41943040 | tf_op jit(solution)/shard_map/all_to_all | solution.py:97
  192.3 0.1 reshape.288
  192.4 0.1 copy.34
  192.6 0.5 broadcast.134
  193.1 1.1 slice_multiply_fusion.6
  194.1 0.1 mul.285
  194.2 0.1 squeeze.18
  194.3 0.1 bitcast_subtract_fusion
  194.3 0.1 maximum_reduce_fusion
  194.6 0.1 dynamic_slice.22
  194.6 0.1 copy_bitcast_fusion.1
  194.7 0.1 fusion.35
  194.8 446.1 %all-to-all-done = bf16[4,5,1,512,1024]{4,3,1,2,0:T(8,128)(2,1)} async-done(((bf16[4,5,1,512,1024]{4,3,1,2,0:T(8,128)(2,1)}), bf16[4,5,1,512,1024]{4,3,1,2,0:T(8,128)(2,1)}, u32[]{:S(2)}, u32[]{:S(2)}) %all-to-all-start) | async-done | bytes 20971552 | tf_op jit(solution)/shard_map/all_to_all | solution.py:97
  640.9 16.0 %fusion = f32[5,512,1024]{2,1,0:T(8,128)} fusion(bf16[4,5,1,512,1024]{4,3,1,2,0:T(8,128)(2,1)} %all-to-all-done), kind=kLoop, calls=%fused_computation.2 | loop fusion | flops 18350080 | bytes 31457280 | tf_op jit(solution)/shard_map/reduce_sum | solution.py:106
  657.0 7.0 fusion.28
  664.0 0.7 copy-done
  664.7 23.2 %fusion.1 = f32[5,4,512,1024]{3,2,0,1:T(8,128)} fusion(bf16[4,5,1,512,1024]{4,3,1,2,0:T(8,128)(2,1)} %all-to-all-done, f32[5,512,1024]{2,1,0:T(8,128)S(1)} %copy-done), kind=kLoop, calls=%fused_computation.3 | loop fusion | flops 20971520 | bytes 73400320 | tf_op jit(solution)/shard_map/sub | solution.py:107
  688.0 19.9 %fusion.46 = (f32[512,1024]{1,0:T(8,128)S(1)}, f32[4,512,1024]{2,1,0:T(8,128)}) fusion(f32[4,1024]{1,0:T(4,128)S(1)} %bitcast.81, f32[4,512]{1,0:T(4,128)S(1)} %fusion.35, f32[5,4,512,1024]{3,2,0,1:T(8,128)} %fusion.1), kind=kLoop, calls=%fused_computation.92 | loop fusion | flops 20447232 | bytes 52453376 | tf_op jit(solution)/shard_map/reduce_sum | solution.py:122
  707.9 0.2 broadcast_multiply_fusion
  708.1 5.1 multiply_reduce_fusion
  713.2 0.5 multiply_sqrt_fusion
  713.7 2.8 sqrt.22
  716.5 3.0 div.75
  719.5 2.6 rsqrt_multiply_fusion
  (22 shorter events, 0.3 us)
Async XLA Ops:
  7.2 118.2 %all-gather.8.cloned.1.call-start = ((), (), s32[]{:S(2)}) async-start(), calls=%async_computation.2 | async-start | bytes 3145728 | tf_op jit(solution)/shard_map/all_gather | solution.py:72
  7.9 117.5 %all-gather.6.cloned.1.call-start = ((), (), s32[]{:S(2)}) async-start(), calls=%async_computation.1 | async-start | bytes 5242880 | tf_op jit(solution)/shard_map/all_gather | solution.py:78
  125.4 10.9 %copy-start.1 = (f32[1024]{0:T(1024)S(1)}, f32[1024]{0:T(1024)}, u32[]{:S(2)}) copy-start(f32[1024]{0:T(1024)} %param.2) | copy-start | bytes 12292
  125.4 10.9 %copy-start.2 = (bf16[1024,2048]{1,0:T(8,128)(2,1)S(1)}, bf16[1024,2048]{1,0:T(8,128)(2,1)}, u32[]{:S(2)}) copy-start(bf16[1024,2048]{1,0:T(8,128)(2,1)} %all-gather.6.cloned.1.call-done) | copy-start | bytes 12582916
  125.4 10.9 %copy-start.3 = (bf16[1024,1024]{1,0:T(8,128)(2,1)S(1)}, bf16[1024,1024]{1,0:T(8,128)(2,1)}, u32[]{:S(2)}) copy-start(bf16[1024,1024]{1,0:T(8,128)(2,1)} %all-gather.8.cloned.1.call-done) | copy-start | bytes 6291460
  184.3 456.7 %all-to-all-start = ((bf16[4,5,1,512,1024]{4,3,1,2,0:T(8,128)(2,1)}), bf16[4,5,1,512,1024]{4,3,1,2,0:T(8,128)(2,1)}, u32[]{:S(2)}, u32[]{:S(2)}) async-start(bf16[4,5,1,512,1024]{4,3,1,2,0:T(8,128)(2,1)} %pad_maximum_fusion), calls=%async_computation | async-start | bytes 41943040 | tf_op jit(solution)/shard_map/all_to_all | solution.py:97
  657.0 7.8 %copy-start = (f32[5,512,1024]{2,1,0:T(8,128)S(1)}, f32[5,512,1024]{2,1,0:T(8,128)}, u32[]{:S(2)}) copy-start(f32[5,512,1024]{2,1,0:T(8,128)} %fusion) | copy-start | bytes 31457284
Sparse Core Ops, SparseCore 0:
  9.5 13.2 all-gather.7
  24.7 54.8 all-gather.5
